TPU v7x, 256 devices: a whole 4x4x8 slice. The times are simulated.
256 devices in a mesh: rep: 2 (over z_hi), dp: 32 (over z_lo, x, core), mp: 4 (over y).
Axes of the slice: x: 4, y: 4, z: 8 (z_hi: 2, z_lo: 4; z = z_hi * 4 + z_lo), core: 2. Of those that a mesh axis runs over, the one named last changes fastest.
Arguments:
- tokens: bfloat16 [24576, 2048], P(('rep', 'dp', 'mp')), may hold values from -6 to 6
- request_ids: int32 [64, 384], P(('rep', 'dp')), may hold values from 0 to 7, never falling along the last dimension, each value on 1 to 192 neighbouring positions
- cache_entries: bfloat16 [32768, 4096], P(('rep', 'dp', 'mp')), may hold values from -250 to 250, as said below
- cached_lengths: int32 [64, 8], replicated, may hold values from 1 to 256, 512 in all within a row
- traded: int32 [32], P('dp'), may hold values from 0 to 1, as said below
- query_weight: bfloat16 [2048, 2048], P(None, 'mp'), may hold values from -0.125 to 0.125
- key_weight: bfloat16 [2048, 2048], P(None, 'mp'), may hold values from -0.125 to 0.125
- value_weight: bfloat16 [2048, 2048], P(None, 'mp'), may hold values from -0.125 to 0.125
- output_weight: bfloat16 [2048, 2048], P('mp'), may hold values from -0.125 to 0.125
- gate_weight: bfloat16 [2048, 8192], P('dp', 'mp'), may hold values from -0.125 to 0.125
- up_weight: bfloat16 [2048, 8192], P('dp', 'mp'), may hold values from -0.125 to 0.125
- down_weight: bfloat16 [2048, 8192], P('dp', 'mp'), may hold values from -0.0625 to 0.0625
Outputs:
- layer_output: bfloat16 [24576, 2048], P(('rep', 'dp', 'mp'))
Inputs may be any that keep to these rules, and one draw needn't show every extreme that they name: `request_ids`: each group's row never falls; every request 0 to 7 has 1 to 192 new tokens in each group, some request exactly 192. `cached_lengths`: each row sums to 512; its largest entry is 256. `traded`: exactly 16 entries are 1. `cache_entries`: keys are stored already rotated to their positions; rows of cache group g are g * 512 to (g + 1) * 512 - 1, the requests' prefixes in request order.
All inputs are finite; a program needn't handle non-finite values.
Results may differ from a plain program's by a relative error of at most 0.013.
The roundings to bfloat16 on the way count: a program that leaves them out, or rounds other values in their place, can miss the bound.
Values may be sent and summed in bfloat16 or wider, within the bound.
A program may use at most 128 MiB of HBM per device.

v0:
```python
import math
import jax
import jax.numpy as jnp
from jax import lax
from jax.sharding import PartitionSpec as P

D = 2048
HEADS = 16
HEAD_DIM = 128
TOK_GROUP = 384
CACHE = 512
EPSILON = 1e-05
ROPE_BASE = 10000.0


def swapped(value, axis, apart):
    mask = 2**apart
    pairs = [(source, source ^ mask) for source in range(lax.axis_size(axis))]
    return lax.ppermute(value, axis, pairs)


def layer_norm(rows):
    center = rows - jnp.mean(rows, axis=-1, keepdims=True)
    spread = jnp.mean(center * center, axis=-1, keepdims=True)
    return center * lax.rsqrt(spread + EPSILON)


def request_layout(request_row, length_row, cache_size):
    number = length_row.shape[0]
    labels = jnp.arange(number, dtype=jnp.int32)
    onehot = (request_row[:, None] == labels[None, :]).astype(jnp.int32)
    counts = jnp.sum(onehot, axis=0)
    starts = jnp.cumsum(counts) - counts
    token_place = jnp.arange(request_row.shape[0], dtype=jnp.int32)
    positions = jnp.sum(onehot * (length_row - starts)[None, :], axis=1) + token_place
    bounds = jnp.cumsum(length_row)
    cache_place = jnp.arange(cache_size, dtype=jnp.int32)
    owner = jnp.sum((cache_place[:, None] >= bounds[None, :]).astype(jnp.int32), axis=1)
    return (positions, owner)


def rotate(vectors, positions):
    half = vectors.shape[-1] // 2
    freq = ROPE_BASE ** (-jnp.arange(half, dtype=jnp.float32) / half)
    angle = positions.astype(jnp.float32)[:, None] * freq[None, :]
    cosine = jnp.cos(angle)[:, None, :]
    sine = jnp.sin(angle)[:, None, :]
    first = vectors[..., :half]
    second = vectors[..., half:]
    return jnp.concatenate(
        [first * cosine - second * sine, second * cosine + first * sine], axis=-1
    )


def attend(query, keys_new, values_new, keys_cache, values_cache, request_row, owner):
    scale = 1.0 / math.sqrt(query.shape[-1])
    keys = jnp.concatenate([keys_cache, keys_new], axis=0)
    values = jnp.concatenate([values_cache, values_new], axis=0)
    scores = jnp.einsum("thd,khd->htk", query, keys, preferred_element_type=jnp.float32) * scale
    count = request_row.shape[0]
    place = jnp.arange(count, dtype=jnp.int32)
    same_cache = owner[None, :] == request_row[:, None]
    same_new = (request_row[None, :] == request_row[:, None]) & (place[None, :] <= place[:, None])
    allowed = jnp.concatenate([same_cache, same_new], axis=1)
    scores = jnp.where(allowed[None], scores, -1e30)
    top = jnp.max(scores, axis=-1, keepdims=True)
    raised = jnp.exp(scores - top)
    total = jnp.sum(raised, axis=-1, keepdims=True)
    weights = (raised / total).astype(jnp.bfloat16)
    mixed = jnp.einsum("htk,khd->thd", weights, values, preferred_element_type=jnp.float32)
    return mixed.astype(jnp.bfloat16)


def local(
    tokens,
    request_ids,
    cache_entries,
    cached_lengths,
    traded,
    query_weight,
    key_weight,
    value_weight,
    output_weight,
    gate_weight,
    up_weight,
    down_weight,
):
    tensor_size = lax.axis_size("mp")
    local_heads = HEADS // tensor_size
    replica = lax.axis_index("rep")
    within = lax.axis_index("dp")
    pairs = lax.axis_size("dp")
    group = replica * pairs + within
    moved_here = traded[0] == 1
    source = jnp.where(moved_here, (1 - replica) * pairs + within, group)
    length_row = lax.dynamic_slice_in_dim(cached_lengths, source, 1, 0)[0]
    request_row = request_ids[0]
    partner = swapped(cache_entries, "rep", 0)
    stored = jnp.where(moved_here, partner, cache_entries)
    by_heads = lax.all_to_all(
        stored.reshape(stored.shape[0], 2, D), "mp", split_axis=2, concat_axis=0, tiled=True
    )
    keys_cache = by_heads[:, 0].reshape(CACHE, local_heads, HEAD_DIM)
    values_cache = by_heads[:, 1].reshape(CACHE, local_heads, HEAD_DIM)
    rows_full = lax.all_gather(tokens, "mp", axis=0, tiled=True)
    positions, owner = request_layout(request_row, length_row, CACHE)
    normed = layer_norm(rows_full.astype(jnp.float32)).astype(jnp.bfloat16)
    query = jnp.dot(normed, query_weight, preferred_element_type=jnp.float32).reshape(
        TOK_GROUP, local_heads, HEAD_DIM
    )
    query = rotate(query, positions).astype(jnp.bfloat16)
    keys_new = jnp.dot(normed, key_weight, preferred_element_type=jnp.float32).reshape(
        TOK_GROUP, local_heads, HEAD_DIM
    )
    keys_new = rotate(keys_new, positions).astype(jnp.bfloat16)
    values_new = (
        jnp.dot(normed, value_weight, preferred_element_type=jnp.float32)
        .astype(jnp.bfloat16)
        .reshape(TOK_GROUP, local_heads, HEAD_DIM)
    )
    mixed = attend(query, keys_new, values_new, keys_cache, values_cache, request_row, owner)
    mixed = mixed.reshape(TOK_GROUP, local_heads * HEAD_DIM)
    own_sum = lax.psum_scatter(
        jnp.dot(mixed, output_weight, preferred_element_type=jnp.float32),
        "mp",
        scatter_dimension=0,
        tiled=True,
    )
    state_own = (tokens.astype(jnp.float32) + own_sum).astype(jnp.bfloat16)
    normed_own = layer_norm(state_own.astype(jnp.float32)).astype(jnp.bfloat16)
    normed_two = lax.all_gather(normed_own, "mp", axis=0, tiled=True)

    def add_rows(piece):
        return jnp.dot(normed_two, piece, preferred_element_type=jnp.float32)

    gate = add_rows(lax.all_gather(gate_weight, "dp", axis=0, tiled=True))
    upward = add_rows(lax.all_gather(up_weight, "dp", axis=0, tiled=True))
    activated = (jax.nn.silu(gate) * upward).astype(jnp.bfloat16)
    terms = lax.dot_general(
        activated,
        lax.all_gather(down_weight, "dp", axis=0, tiled=True),
        (((1,), (1,)), ((), ())),
        preferred_element_type=jnp.float32,
    )
    hidden_own = lax.psum_scatter(terms, "mp", scatter_dimension=0, tiled=True)
    return (state_own.astype(jnp.float32) + hidden_own).astype(jnp.bfloat16)


def solution(mesh):
    in_specs = (
        P(("rep", "dp", "mp"), None),
        P(("rep", "dp"), None),
        P(("rep", "dp", "mp"), None),
        P(),
        P("dp"),
        P(None, "mp"),
        P(None, "mp"),
        P(None, "mp"),
        P("mp", None),
        P("dp", "mp"),
        P("dp", "mp"),
        P("dp", "mp"),
    )
    out_specs = P(("rep", "dp", "mp"), None)
    return jax.shard_map(local, mesh=mesh, in_specs=in_specs, out_specs=out_specs, check_vma=False)
```

profile of v0, /device:TPU:1, one launch (start us, length us, event | category | flops | bytes accessed | tf_op | source)
XLA Modules:
  0.0 476.3 jit_solution(9177185737929228484)
XLA Ops:
  6.5 1.8 copy.71
  8.3 7.8 %collective-permute-start = (bf16[128,4096]{0,1:T(8,128)(2,1)S(1)}, bf16[128,4096]{0,1:T(8,128)(2,1)}, u32[]{:S(2)}, u32[]{:S(2)}) collective-permute-start(bf16[128,4096]{0,1:T(8,128)(2,1)S(1)} %copy.71), channel_id=1, source_target_pairs={{0,128},{128,0},{1,129},{129,1},{2,130},{130,2},{3,131},{131,3},{4... | collective-permute-start | bytes 3145736 | tf_op jit(solution)/shard_map/ppermute | solution.py:19
  19.2 25.3 %collective-permute-done = bf16[128,4096]{0,1:T(8,128)(2,1)} collective-permute-done((bf16[128,4096]{0,1:T(8,128)(2,1)S(1)}, bf16[128,4096]{0,1:T(8,128)(2,1)}, u32[]{:S(2)}, u32[]{:S(2)}) %collective-permute-start) | collective-permute-done | bytes 1048608 | tf_op jit(solution)/shard_map/ppermute | solution.py:19
  44.6 1.3 broadcast_select_fusion
  45.9 9.5 %copy.73 = bf16[128,2,2048]{0,1,2:T(2,128)(2,1)} copy(bf16[128,2,2048]{0,2,1:T(8,128)(2,1)S(1)} %bitcast.28) | data formatting | bytes 2097152 | tf_op jit(solution)/shard_map/reshape | solution.py:101
  55.4 4.7 all-to-all-start
  61.0 1.5 multiply_cosine_fusion
  62.5 7.3 %all-to-all-done = bf16[128,2,2048]{0,1,2:T(2,128)(2,1)S(1)} async-done(((bf16[128,2,2048]{0,1,2:T(2,128)(2,1)}), bf16[128,2,2048]{0,1,2:T(2,128)(2,1)S(1)}, u32[]{:S(2)}, u32[]{:S(2)}) %all-to-all-start) | async-done | bytes 1048608 | tf_op jit(solution)/shard_map/all_to_all | solution.py:100
  70.9 1.5 copy.75
  73.5 1.3 copy.81
  75.0 2.0 copy.76
  77.0 1.8 convert_reduce_fusion
  78.9 2.0 fusion.4
  80.8 3.6 fusion.35
  84.4 1.4 reshape.153
  85.8 4.0 fusion.37
  89.8 2.3 reshape.151
  92.1 3.9 convolution_convert_fusion
  95.9 1.9 copy.85
  97.8 2.3 fusion.41
  101.6 2.7 fusion.43
  105.4 2.7 fusion.44
  108.4 61.6 %reduce-scatter.3.cloned.1.call-done = f32[96,2048]{1,0:T(8,128)} async-done(((f32[384,2048]{1,0:T(8,128)}), f32[96,2048]{1,0:T(8,128)}) %reduce-scatter.3.cloned.1.call-update) | async-done | bytes 786448 | tf_op jit(solution)/shard_map/reduce_scatter | solution.py:123
  169.9 1.3 convert_reduce_fusion.1
  174.4 27.1 %all-gather.8.cloned.1.call-done = bf16[384,2048]{1,0:T(8,128)(2,1)} async-done(((bf16[96,2048]{1,0:T(8,128)(2,1)}), bf16[384,2048]{1,0:T(8,128)(2,1)}) %all-gather.8.cloned.1.call-update) | async-done | bytes 1572880 | tf_op jit(solution)/shard_map/all_gather | solution.py:131
  201.5 71.4 %all-gather.10.cloned.1.call-done = bf16[2048,2048]{1,0:T(8,128)(2,1)} async-done(((bf16[64,2048]{1,0:T(8,128)(2,1)}), bf16[2048,2048]{1,0:T(8,128)(2,1)}) %all-gather.10.cloned.1.call-update) | async-done | bytes 8388624 | tf_op jit(solution)/shard_map/all_gather | solution.py:136
  272.9 9.0 %fusion.45 = f32[384,2048]{1,0:T(8,128)} fusion(bf16[384,2048]{1,0:T(8,128)(2,1)} %all-gather.8.cloned.1.call-done, bf16[2048,2048]{1,0:T(8,128)(2,1)} %all-gather.10.cloned.1.call-done), kind=kOutput, calls=%fused_computation.76 | convolution fusion | flops 3221225472 | bytes 13107200 | tf_op jit(solution)/shard_map/dot_general | solution.py:134
  281.9 60.6 %all-gather.12.cloned.1.call-done = bf16[2048,2048]{1,0:T(8,128)(2,1)} async-done(((bf16[64,2048]{1,0:T(8,128)(2,1)}), bf16[2048,2048]{1,0:T(8,128)(2,1)}) %all-gather.12.cloned.1.call-update) | async-done | bytes 8388624 | tf_op jit(solution)/shard_map/all_gather | solution.py:137
  342.5 69.7 %all-gather.14.cloned.1.call-done = bf16[2048,2048]{1,0:T(8,128)(2,1)} async-done(((bf16[64,2048]{1,0:T(8,128)(2,1)}), bf16[2048,2048]{1,0:T(8,128)(2,1)}) %all-gather.14.cloned.1.call-update) | async-done | bytes 8388624 | tf_op jit(solution)/shard_map/all_gather | solution.py:141
  412.2 15.9 %fusion.25 = f32[384,2048]{1,0:T(8,128)} fusion(bf16[2048,2048]{1,0:T(8,128)(2,1)} %all-gather.14.cloned.1.call-done, f32[384,2048]{1,0:T(8,128)} %fusion.45, bf16[384,2048]{1,0:T(8,128)(2,1)} %all-gather.8.cloned.1.call-done, bf16[2048,2048]{1,0:T(8,128)(2,1)} %all-gather.12.cloned.1.call-done), kind=kOutput, calls=%fused_computation.42 | convolution fusion | flops 6447169536 | bytes 24641536 | tf_op jit(solution)/shard_map/dot_general | solution.py:139
  428.1 39.4 %reduce-scatter.5.cloned.1.call-done = f32[96,2048]{1,0:T(8,128)} async-done(((f32[384,2048]{1,0:T(8,128)}), f32[96,2048]{1,0:T(8,128)}) %reduce-scatter.5.cloned.1.call-update) | async-done | bytes 786448 | tf_op jit(solution)/shard_map/reduce_scatter | solution.py:145
  467.5 2.0 fusion.24
  (59 shorter events, 11.5 us)
Async XLA Ops:
  6.5 98.8 %copy-start = (bf16[512,2048]{1,0:T(8,128)(2,1)S(1)}, bf16[512,2048]{1,0:T(8,128)(2,1)}, u32[]{:S(2)}) copy-start(bf16[512,2048]{1,0:T(8,128)(2,1)} %param.20) | copy-start | bytes 6291460
  6.5 70.5 %all-gather.6.cloned.1.call-start = ((), (), s32[]{:S(2)}) async-start(), calls=%async_computation.3 | async-start | bytes 1966080 | tf_op jit(solution)/shard_map/all_gather | solution.py:105
  8.3 36.3 %collective-permute-start = (bf16[128,4096]{0,1:T(8,128)(2,1)S(1)}, bf16[128,4096]{0,1:T(8,128)(2,1)}, u32[]{:S(2)}, u32[]{:S(2)}) collective-permute-start(bf16[128,4096]{0,1:T(8,128)(2,1)S(1)} %copy.71), channel_id=1, source_target_pairs={{0,128},{128,0},{1,129},{129,1},{2,130},{130,2},{3,131},{131,3},{4... | collective-permute-start | bytes 3145736 | tf_op jit(solution)/shard_map/ppermute | solution.py:19
  55.4 14.5 %all-to-all-start = ((bf16[128,2,2048]{0,1,2:T(2,128)(2,1)}), bf16[128,2,2048]{0,1,2:T(2,128)(2,1)S(1)}, u32[]{:S(2)}, u32[]{:S(2)}) async-start(bf16[128,2,2048]{0,1,2:T(2,128)(2,1)} %copy.73), calls=%async_computation | async-start | bytes 2097152 | tf_op jit(solution)/shard_map/all_to_all | solution.py:100
  60.1 109.8 %reduce-scatter.3.cloned.1.call-start = ((), (), s32[]{:S(2)}) async-start(), calls=%async_computation.4 | async-start | bytes 3932160 | tf_op jit(solution)/shard_map/reduce_scatter | solution.py:123
  77.0 3.8 copy-start.2
  97.8 2.3 copy-start.4
  97.8 2.3 copy-start.5
  100.6 1.0 copy-start.8
  101.6 2.7 copy-start.6
  101.6 2.7 copy-start.7
  105.4 64.5 %copy-start.3 = (bf16[96,2048]{1,0:T(8,128)(2,1)S(1)}, bf16[96,2048]{1,0:T(8,128)(2,1)}, u32[]{:S(2)}) copy-start(bf16[96,2048]{1,0:T(8,128)(2,1)} %param.12) | copy-start | bytes 1179652
  108.1 93.4 %all-gather.8.cloned.1.call-start = ((), (), s32[]{:S(2)}) async-start(), calls=%async_computation.5 | async-start | bytes 1966080 | tf_op jit(solution)/shard_map/all_gather | solution.py:131
  172.6 100.3 %all-gather.10.cloned.1.call-start = ((), (), s32[]{:S(2)}) async-start(), calls=%async_computation.6 | async-start | bytes 8650752 | tf_op jit(solution)/shard_map/all_gather | solution.py:136
  173.1 169.4 %all-gather.12.cloned.1.call-start = ((), (), s32[]{:S(2)}) async-start(), calls=%async_computation.7 | async-start | bytes 8650752 | tf_op jit(solution)/shard_map/all_gather | solution.py:137
  173.7 238.5 %all-gather.14.cloned.1.call-start = ((), (), s32[]{:S(2)}) async-start(), calls=%async_computation.8 | async-start | bytes 8650752 | tf_op jit(solution)/shard_map/all_gather | solution.py:141
  174.3 293.2 %reduce-scatter.5.cloned.1.call-start = ((), (), s32[]{:S(2)}) async-start(), calls=%async_computation.9 | async-start | bytes 3932160 | tf_op jit(solution)/shard_map/reduce_scatter | solution.py:145
  412.2 57.2 %copy-start.1 = (bf16[512,2048]{1,0:T(8,128)(2,1)S(1)}, bf16[512,2048]{1,0:T(8,128)(2,1)}, u32[]{:S(2)}) copy-start(bf16[512,2048]{1,0:T(8,128)(2,1)} %param.20) | copy-start | bytes 6291460
Sparse Core Ops, SparseCore 0:
  16.3 27.0 all-gather.5
  108.2 61.6 reduce-scatter.2
  172.7 28.7 all-gather.7
  203.2 69.6 all-gather.9
  274.6 67.9 all-gather.11
  344.2 67.9 all-gather.13
  428.2 39.2 reduce-scatter.4
where the time goes:
time: 477 us; the launch traced here: 476 us
  waiting for transfers between devices  364 us (76%)
  matrix products  41 us (9%)
  local copies, waits for them, and re-layouts  27.2 us (6%)
  other arithmetic  16.8 us (4%)
  between operations  14.3 us (3%)
  starting transfers between devices  13 us (3%)
    all_gather x1, waiting for transfers between devices, local(): gate = add_rows(lax.all_gather(gate_weight, 'dp', axis=0, tiled=True))  71.4 us
    all_gather x1, waiting for transfers between devices, local(): lax.all_gather(down_weight, 'dp', axis=0, tiled=True)  69.7 us
    reduce_scatter x1, waiting for transfers between devices, local(): lax.psum_scatter(jnp.dot(mixed, output_weight, preferred_element_type=jnp...  61.6 us
    all_gather x1, waiting for transfers between devices, local(): upward = add_rows(lax.all_gather(up_weight, 'dp', axis=0, tiled=True))  60.6 us
    reduce_scatter x1, waiting for transfers between devices, local(): hidden_own = lax.psum_scatter(terms, 'mp', scatter_dimension=0, tiled=True)  39.4 us
    all_gather x1, waiting for transfers between devices, local(): normed_two = lax.all_gather(normed_own, 'mp', axis=0, tiled=True)  27.1 us
    ppermute x1, waiting for transfers between devices, swapped(): return lax.ppermute(value, axis, pairs)  25.3 us
    dot_general x1, matrix products, local(): lax.dot_general(activated, lax.all_gather(down_weight, 'dp', axis=0, tile...  15.9 us
  transfers between devices with their start and end apart: 9, of which 8 were waited for; matrix products, arithmetic and copies ran while one was open for 7% of the time, Pallas kernels for 0%

commit v1 on v0

--- a/solution.py
+++ b/solution.py
@@ -134,7 +134,11 @@
         return jnp.dot(normed_two, piece, preferred_element_type=jnp.float32)
 
     gate = add_rows(lax.all_gather(gate_weight, "dp", axis=0, tiled=True))
-    upward = add_rows(lax.all_gather(up_weight, "dp", axis=0, tiled=True))
+    upward = add_rows(
+        jnp.concatenate(
+            lax.all_to_all(jnp.stack([up_weight] * lax.axis_size("dp")), "dp", 0, 0), axis=0
+        )
+    )
     activated = (jax.nn.silu(gate) * upward).astype(jnp.bfloat16)
     terms = lax.dot_general(
         activated,

time: 477 us -> 524 us (1.099)
  waiting for transfers between devices: 364 us -> 399 us
  starting transfers between devices: 13 us -> 21 us
    all_gather x1, waiting for transfers between devices: 71.4 us -> 175 us  [local(): gate = add_rows(lax.all_gather(gate_weight, 'dp', axis=0, tiled=True))]
    all_gather x1 -> x0, waiting for transfers between devices: 60.6 us -> none  [local(): upward = add_rows(lax.all_gather(up_weight, 'dp', axis=0, tiled=True))]
    all_to_all x0 -> x1, waiting for transfers between devices: none -> 48.5 us  [local(): lax.all_to_all(jnp.stack([up_weight] * lax.axis_size('dp')), 'dp', 0, 0)]
    all_gather x1, waiting for transfers between devices: 69.7 us -> 27.1 us  [local(): lax.all_gather(down_weight, 'dp', axis=0, tiled=True)]
    all_gather x1, waiting for transfers between devices: 27.1 us -> 15.4 us  [local(): normed_two = lax.all_gather(normed_own, 'mp', axis=0, tiled=True)]
    all_to_all x0 -> x1, starting transfers between devices: none -> 8.04 us  [local(): lax.all_to_all(jnp.stack([up_weight] * lax.axis_size('dp')), 'dp', 0, 0)]
where the time goes in v1:
time: 524 us; the launch traced here: 523 us
  waiting for transfers between devices  399 us (76%)
  matrix products  40.8 us (8%)
  local copies, waits for them, and re-layouts  31.5 us (6%)
  starting transfers between devices  21 us (4%)
  other arithmetic  16.8 us (3%)
  between operations  14.3 us (3%)
    all_gather x1, waiting for transfers between devices, local(): gate = add_rows(lax.all_gather(gate_weight, 'dp', axis=0, tiled=True))  175 us
    reduce_scatter x1, waiting for transfers between devices, local(): lax.psum_scatter(jnp.dot(mixed, output_weight, preferred_element_type=jnp...  61.6 us
    all_to_all x1, waiting for transfers between devices, local(): lax.all_to_all(jnp.stack([up_weight] * lax.axis_size('dp')), 'dp', 0, 0)  48.5 us
    reduce_scatter x1, waiting for transfers between devices, local(): hidden_own = lax.psum_scatter(terms, 'mp', scatter_dimension=0, tiled=True)  37.7 us
    all_gather x1, waiting for transfers between devices, local(): lax.all_gather(down_weight, 'dp', axis=0, tiled=True)  27.1 us
    ppermute x1, waiting for transfers between devices, swapped(): return lax.ppermute(value, axis, pairs)  25.3 us
    dot_general x1, matrix products, local(): lax.dot_general(activated, lax.all_gather(down_weight, 'dp', axis=0, tile...  15.9 us
    all_gather x1, waiting for transfers between devices, local(): normed_two = lax.all_gather(normed_own, 'mp', axis=0, tiled=True)  15.4 us
  transfers between devices with their start and end apart: 9, of which 8 were waited for; matrix products, arithmetic and copies ran while one was open for 7% of the time, Pallas kernels for 0%

profile of v1, /device:TPU:1, one launch (start us, length us, event | category | flops | bytes accessed | tf_op | source)
XLA Modules:
  0.0 523.2 jit_solution(1397692109149934248)
XLA Ops:
  6.5 1.8 copy.71
  8.3 7.8 %collective-permute-start = (bf16[128,4096]{0,1:T(8,128)(2,1)S(1)}, bf16[128,4096]{0,1:T(8,128)(2,1)}, u32[]{:S(2)}, u32[]{:S(2)}) collective-permute-start(bf16[128,4096]{0,1:T(8,128)(2,1)S(1)} %copy.71), channel_id=1, source_target_pairs={{0,128},{128,0},{1,129},{129,1},{2,130},{130,2},{3,131},{131,3},{4... | collective-permute-start | bytes 3145736 | tf_op jit(solution)/shard_map/ppermute | solution.py:19
  19.2 25.3 %collective-permute-done = bf16[128,4096]{0,1:T(8,128)(2,1)} collective-permute-done((bf16[128,4096]{0,1:T(8,128)(2,1)S(1)}, bf16[128,4096]{0,1:T(8,128)(2,1)}, u32[]{:S(2)}, u32[]{:S(2)}) %collective-permute-start) | collective-permute-done | bytes 1048608 | tf_op jit(solution)/shard_map/ppermute | solution.py:19
  44.6 1.3 broadcast_select_fusion
  45.9 9.5 %copy.73 = bf16[128,2,2048]{0,1,2:T(2,128)(2,1)} copy(bf16[128,2,2048]{0,2,1:T(8,128)(2,1)S(1)} %bitcast.29) | data formatting | bytes 2097152 | tf_op jit(solution)/shard_map/reshape | solution.py:101
  55.4 4.7 all-to-all-start
  61.0 1.5 multiply_cosine_fusion
  62.5 7.3 %all-to-all-done = bf16[128,2,2048]{0,1,2:T(2,128)(2,1)S(1)} async-done(((bf16[128,2,2048]{0,1,2:T(2,128)(2,1)}), bf16[128,2,2048]{0,1,2:T(2,128)(2,1)S(1)}, u32[]{:S(2)}, u32[]{:S(2)}) %all-to-all-start) | async-done | bytes 1048608 | tf_op jit(solution)/shard_map/all_to_all | solution.py:100
  70.9 1.5 copy.75
  75.0 2.0 copy.76
  77.0 1.8 convert_reduce_fusion
  78.9 2.0 fusion.4
  80.8 3.6 fusion.35
  84.4 1.4 reshape.158
  85.8 4.0 fusion.37
  89.8 2.3 reshape.156
  92.1 3.9 convolution_convert_fusion
  95.9 1.9 copy.85
  97.8 2.3 fusion.41
  101.6 2.7 fusion.43
  105.4 2.7 fusion.44
  108.4 61.6 %reduce-scatter.3.cloned.1.call-done = f32[96,2048]{1,0:T(8,128)} async-done(((f32[384,2048]{1,0:T(8,128)}), f32[96,2048]{1,0:T(8,128)}) %reduce-scatter.3.cloned.1.call-update) | async-done | bytes 786448 | tf_op jit(solution)/shard_map/reduce_scatter | solution.py:123
  173.2 4.3 stack.2
  177.4 8.0 %all-to-all-start.1 = ((bf16[32,64,2048]{2,1,0:T(8,128)(2,1)}), bf16[32,64,2048]{2,1,0:T(8,128)(2,1)}, u32[]{:S(2)}, u32[]{:S(2)}) async-start(bf16[32,64,2048]{2,1,0:T(8,128)(2,1)} %stack.2), calls=%async_computation.2 | async-start | bytes 16777216 | tf_op jit(solution)/shard_map/all_to_all | solution.py:139
  186.1 15.4 %all-gather.7.cloned.1.call-done = bf16[384,2048]{1,0:T(8,128)(2,1)} async-done(((bf16[96,2048]{1,0:T(8,128)(2,1)}), bf16[384,2048]{1,0:T(8,128)(2,1)}) %all-gather.7.cloned.1.call-update) | async-done | bytes 1572880 | tf_op jit(solution)/shard_map/all_gather | solution.py:131
  201.5 174.8 %all-gather.9.cloned.1.call-done = bf16[2048,2048]{1,0:T(8,128)(2,1)} async-done(((bf16[64,2048]{1,0:T(8,128)(2,1)}), bf16[2048,2048]{1,0:T(8,128)(2,1)}) %all-gather.9.cloned.1.call-update) | async-done | bytes 8388624 | tf_op jit(solution)/shard_map/all_gather | solution.py:136
  376.3 8.9 %fusion.45 = f32[384,2048]{1,0:T(8,128)} fusion(bf16[384,2048]{1,0:T(8,128)(2,1)} %all-gather.7.cloned.1.call-done, bf16[2048,2048]{1,0:T(8,128)(2,1)} %all-gather.9.cloned.1.call-done), kind=kOutput, calls=%fused_computation.76 | convolution fusion | flops 3221225472 | bytes 13107200 | tf_op jit(solution)/shard_map/dot_general | solution.py:134
  385.2 48.5 %all-to-all-done.1 = bf16[32,64,2048]{2,1,0:T(8,128)(2,1)} async-done(((bf16[32,64,2048]{2,1,0:T(8,128)(2,1)}), bf16[32,64,2048]{2,1,0:T(8,128)(2,1)}, u32[]{:S(2)}, u32[]{:S(2)}) %all-to-all-start.1) | async-done | bytes 8388640 | tf_op jit(solution)/shard_map/all_to_all | solution.py:139
  433.7 27.1 %all-gather.11.cloned.1.call-done = bf16[2048,2048]{1,0:T(8,128)(2,1)} async-done(((bf16[64,2048]{1,0:T(8,128)(2,1)}), bf16[2048,2048]{1,0:T(8,128)(2,1)}) %all-gather.11.cloned.1.call-update) | async-done | bytes 8388624 | tf_op jit(solution)/shard_map/all_gather | solution.py:145
  460.8 15.9 %fusion.25 = f32[384,2048]{1,0:T(8,128)} fusion(bf16[2048,2048]{1,0:T(8,128)(2,1)} %all-gather.11.cloned.1.call-done, f32[384,2048]{1,0:T(8,128)} %fusion.45, bf16[384,2048]{1,0:T(8,128)(2,1)} %all-gather.7.cloned.1.call-done, bf16[2048,2048]{1,0:T(8,128)(2,1)} %bitcast.14), kind=kOutput, calls=%fused_computation.42 | convolution fusion | flops 6447169536 | bytes 24641536 | tf_op jit(solution)/shard_map/dot_general | solution.py:143
  476.7 37.7 %reduce-scatter.5.cloned.1.call-done = f32[96,2048]{1,0:T(8,128)} async-done(((f32[384,2048]{1,0:T(8,128)}), f32[96,2048]{1,0:T(8,128)}) %reduce-scatter.5.cloned.1.call-update) | async-done | bytes 786448 | tf_op jit(solution)/shard_map/reduce_scatter | solution.py:149
  514.4 2.0 fusion.24
  (61 shorter events, 13.5 us)
Async XLA Ops:
  6.5 98.8 %copy-start = (bf16[512,2048]{1,0:T(8,128)(2,1)S(1)}, bf16[512,2048]{1,0:T(8,128)(2,1)}, u32[]{:S(2)}) copy-start(bf16[512,2048]{1,0:T(8,128)(2,1)} %param.20) | copy-start | bytes 6291460
  6.5 70.5 %all-gather.5.cloned.1.call-start = ((), (), s32[]{:S(2)}) async-start(), calls=%async_computation.4 | async-start | bytes 1966080 | tf_op jit(solution)/shard_map/all_gather | solution.py:105
  8.3 36.3 %collective-permute-start = (bf16[128,4096]{0,1:T(8,128)(2,1)S(1)}, bf16[128,4096]{0,1:T(8,128)(2,1)}, u32[]{:S(2)}, u32[]{:S(2)}) collective-permute-start(bf16[128,4096]{0,1:T(8,128)(2,1)S(1)} %copy.71), channel_id=1, source_target_pairs={{0,128},{128,0},{1,129},{129,1},{2,130},{130,2},{3,131},{131,3},{4... | collective-permute-start | bytes 3145736 | tf_op jit(solution)/shard_map/ppermute | solution.py:19
  55.4 14.5 %all-to-all-start = ((bf16[128,2,2048]{0,1,2:T(2,128)(2,1)}), bf16[128,2,2048]{0,1,2:T(2,128)(2,1)S(1)}, u32[]{:S(2)}, u32[]{:S(2)}) async-start(bf16[128,2,2048]{0,1,2:T(2,128)(2,1)} %copy.73), calls=%async_computation | async-start | bytes 2097152 | tf_op jit(solution)/shard_map/all_to_all | solution.py:100
  60.1 109.8 %reduce-scatter.3.cloned.1.call-start = ((), (), s32[]{:S(2)}) async-start(), calls=%async_computation.5 | async-start | bytes 3932160 | tf_op jit(solution)/shard_map/reduce_scatter | solution.py:123
  77.0 3.8 copy-start.2
  97.8 2.3 copy-start.4
  97.8 2.3 copy-start.5
  100.6 1.0 copy-start.8
  101.6 2.7 copy-start.6
  101.6 2.7 copy-start.7
  105.4 64.6 %copy-start.3 = (bf16[96,2048]{1,0:T(8,128)(2,1)S(1)}, bf16[96,2048]{1,0:T(8,128)(2,1)}, u32[]{:S(2)}) copy-start(bf16[96,2048]{1,0:T(8,128)(2,1)} %param.12) | copy-start | bytes 1179652
  108.1 65.1 %copy-start.9 = (bf16[64,2048]{1,0:T(8,128)(2,1)S(1)}, bf16[64,2048]{1,0:T(8,128)(2,1)}, u32[]{:S(2)}) copy-start(bf16[64,2048]{1,0:T(8,128)(2,1)} %param.22) | copy-start | bytes 786436
  108.1 93.4 %all-gather.7.cloned.1.call-start = ((), (), s32[]{:S(2)}) async-start(), calls=%async_computation.6 | async-start | bytes 1966080 | tf_op jit(solution)/shard_map/all_gather | solution.py:131
  172.6 203.7 %all-gather.9.cloned.1.call-start = ((), (), s32[]{:S(2)}) async-start(), calls=%async_computation.7 | async-start | bytes 8650752 | tf_op jit(solution)/shard_map/all_gather | solution.py:136
  177.4 256.3 %all-to-all-start.1 = ((bf16[32,64,2048]{2,1,0:T(8,128)(2,1)}), bf16[32,64,2048]{2,1,0:T(8,128)(2,1)}, u32[]{:S(2)}, u32[]{:S(2)}) async-start(bf16[32,64,2048]{2,1,0:T(8,128)(2,1)} %stack.2), calls=%async_computation.2 | async-start | bytes 16777216 | tf_op jit(solution)/shard_map/all_to_all | solution.py:139
  185.5 275.3 %all-gather.11.cloned.1.call-start = ((), (), s32[]{:S(2)}) async-start(), calls=%async_computation.8 | async-start | bytes 8650752 | tf_op jit(solution)/shard_map/all_gather | solution.py:145
  186.1 328.3 %reduce-scatter.5.cloned.1.call-start = ((), (), s32[]{:S(2)}) async-start(), calls=%async_computation.9 | async-start | bytes 3932160 | tf_op jit(solution)/shard_map/reduce_scatter | solution.py:149
  460.8 55.6 %copy-start.1 = (bf16[512,2048]{1,0:T(8,128)(2,1)S(1)}, bf16[512,2048]{1,0:T(8,128)(2,1)}, u32[]{:S(2)}) copy-start(bf16[512,2048]{1,0:T(8,128)(2,1)} %param.20) | copy-start | bytes 6291460
Sparse Core Ops, SparseCore 0:
  16.3 27.0 all-gather.4
  108.2 61.6 reduce-scatter.2
  172.7 28.7 all-gather.6
  203.2 173.0 all-gather.8
  378.0 82.7 all-gather.10
  476.8 37.5 reduce-scatter.4
